TPU v7x, 256 devices: a whole 4x4x8 slice. The times are simulated.
256 devices in a mesh: ctx: 16 (over y, x), exp: 16 (over z, core).
Axes of the slice: x: 4, y: 4, z: 8, core: 2. Of those that a mesh axis runs over, the one named last changes fastest.
Arguments:
- tokens: bfloat16 [2048, 4096], P('ctx', 'exp'), may hold values from -6 to 6
- input_weight: bfloat16 [4096, 8192], P('ctx', 'exp'), may hold values from -0.09375 to 0.09375
- gate_weight: bfloat16 [4096, 8192], P('ctx', 'exp'), may hold values from -0.09375 to 0.09375
- conv_weight: float32 [4, 8192], P(None, 'exp'), may hold values from -3 to 3
- conv_bias: float32 [8192], P('exp'), may hold values from -3 to 3
- state_weight: bfloat16 [8192, 32], P('exp'), may hold values from -0.0078125 to 0.0078125
- step_size: float32 [2048, 8192], P('ctx', 'exp'), may hold values from 0 to 1, as said below
- skip_gain: float32 [8192], P('exp'), may hold values from 0.5 to 2
- output_weight: bfloat16 [8192, 4096], P('exp', 'ctx'), may hold values from -0.0625 to 0.0625
- norm_gain: float32 [4096], replicated, may hold values from 0.1 to 1.9
- router_weight: bfloat16 [4096, 16], replicated, may hold values from -0.09375 to 0.09375
- expert_gate: bfloat16 [16, 7168, 4096], P('exp', 'ctx'), may hold values from -0.09375 to 0.09375
- expert_up: bfloat16 [16, 7168, 4096], P('exp', 'ctx'), may hold values from -0.09375 to 0.09375
- expert_down: bfloat16 [16, 7168, 4096], P('exp', 'ctx'), may hold values from -0.0625 to 0.0625
- expert_ids: int32 [2048, 2], P(('ctx', 'exp')), may hold values from 0 to 15, all different within a row; in each aligned block of 8 rows (0 to 7, 8 to 15, ...) at most 2 rows name the same one
Outputs:
- layer_out: bfloat16 [2048, 4096], P(('ctx', 'exp'))
Inputs may be any that keep to these rules, and one draw needn't show every extreme that they name: `expert_ids`: each token names 2 different experts; in each aligned block of 8 tokens no expert is named by more than 2 tokens. `step_size`: a positive rate for each token and channel.
All inputs are finite; a program needn't handle non-finite values.
Results may differ from a plain program's by a relative error of at most 0.028.
Values may be sent and summed in bfloat16 or wider, within the bound.
A program may use at most 128 MiB of HBM per device.

v0:
```python
import jax
import jax.numpy as jnp
from jax import lax
from jax.sharding import PartitionSpec as P

STATE = 16
CONV = 4
TOP = 2
CAP = 2
precise = lax.Precision.HIGHEST


def shifted(shard, axis, by):
    devices = lax.axis_size(axis)
    pairs = [(i, i + by) for i in range(devices) if 0 <= i + by < devices]
    return lax.ppermute(shard, axis, pairs)


def causal_part(scores, decay_block, input_block):
    length = decay_block.shape[0]
    causal = (jnp.arange(length)[:, None] >= jnp.arange(length)[None, :])[:, :, None]
    distance = decay_block[:, None, :] - decay_block[None, :, :]
    weight = jnp.where(causal, jnp.exp(-jnp.where(causal, distance, 0.0)), 0.0)
    return jnp.einsum("ts,tsc,sc->tc", scores, weight, input_block, precision=precise)


def local(
    tokens,
    input_weight,
    gate_weight,
    conv_weight,
    conv_bias,
    state_weight,
    step_size,
    skip_gain,
    output_weight,
    norm_gain,
    router_weight,
    expert_gate,
    expert_up,
    expert_down,
    expert_ids,
):
    whole_stretch = lax.all_gather(tokens, "exp", axis=1, tiled=True)
    stretch_rows = whole_stretch.shape[0]
    inner_width = input_weight.shape[1]
    inner_x = jnp.dot(
        whole_stretch,
        lax.all_gather(input_weight, "ctx", axis=0, tiled=True),
        preferred_element_type=jnp.float32,
    )
    inner_z = jnp.dot(
        whole_stretch,
        lax.all_gather(gate_weight, "ctx", axis=0, tiled=True),
        preferred_element_type=jnp.float32,
    )
    inner_x = inner_x.astype(jnp.bfloat16)
    inner_z = inner_z.astype(jnp.bfloat16)
    earlier_rows = shifted(inner_x[stretch_rows - (CONV - 1) :], "ctx", 1)
    extended = jnp.concatenate([earlier_rows, inner_x], 0).astype(jnp.float32)
    filtered = jnp.broadcast_to(conv_bias[None, :], (stretch_rows, inner_width))
    for offset in range(CONV):
        filtered = (
            filtered + conv_weight[offset][None, :] * extended[offset : offset + stretch_rows]
        )
    mixer_in = jax.nn.silu(filtered).astype(jnp.bfloat16)
    mixer_wide = mixer_in.astype(jnp.float32)
    projections = lax.psum(
        jnp.dot(mixer_in, state_weight, preferred_element_type=jnp.float32), "exp"
    )
    input_gain = projections[:, :STATE]
    readout = projections[:, STATE:]
    cumulative = jnp.cumsum(step_size, 0)
    scores = jnp.dot(readout, input_gain.T, precision=precise)
    block_width = 128
    block_count = inner_width // block_width
    decay_blocks = cumulative.reshape(stretch_rows, block_count, block_width).transpose(1, 0, 2)
    incoming_slabs = mixer_wide.reshape(stretch_rows, block_count, block_width).transpose(1, 0, 2)
    inside = lax.map(
        lambda paired: causal_part(scores, paired[0], paired[1]), (decay_blocks, incoming_slabs)
    )
    inside = inside.transpose(1, 0, 2).reshape(stretch_rows, inner_width)
    total_decay = cumulative[stretch_rows - 1]
    tail_weight = jnp.exp(-(total_decay[None, :] - cumulative)) * mixer_wide
    local_end = jnp.dot(tail_weight.T, input_gain, precision=precise)
    stretch_keep = jnp.exp(-total_decay)

    def relay_step(turn_index, received):
        leaving = stretch_keep[:, None] * received + local_end
        return shifted(leaving, "ctx", 1)

    entering = lax.fori_loop(0, lax.axis_size("ctx") - 1, relay_step, jnp.zeros_like(local_end))
    carried = jnp.exp(-cumulative) * jnp.dot(readout, entering.T, precision=precise)
    mixed_state = (inside + carried + skip_gain[None, :] * mixer_wide) * jax.nn.silu(
        inner_z.astype(jnp.float32)
    )
    blender_result = mixed_state.astype(jnp.bfloat16)
    row_count = expert_ids.shape[0]
    start_row = lax.axis_index("exp") * row_count
    own_tokens = lax.dynamic_slice_in_dim(whole_stretch, start_row, row_count, 0)
    out_whole = lax.all_gather(output_weight, "ctx", axis=1, tiled=True)
    projected = lax.psum_scatter(
        jnp.dot(blender_result, out_whole, preferred_element_type=jnp.float32).astype(jnp.bfloat16),
        "exp",
        scatter_dimension=0,
        tiled=True,
    ).astype(jnp.float32)
    residual = (own_tokens.astype(jnp.float32) + projected).astype(jnp.bfloat16)
    stream = residual.astype(jnp.float32)
    normed = (
        stream
        * lax.rsqrt(jnp.mean(stream * stream, -1, keepdims=True) + 1e-05)
        * norm_gain[None, :]
    ).astype(jnp.bfloat16)
    logits = jnp.dot(normed, router_weight, preferred_element_type=jnp.float32)
    experts = router_weight.shape[1]
    expert_range = jnp.arange(experts, dtype=jnp.int32)
    chosen = expert_ids[:, :, None] == expert_range[None, None, :]
    selected_entry = jnp.sum(jnp.where(chosen, logits[:, None, :], 0.0), -1)
    shares = jax.nn.sigmoid(selected_entry - selected_entry[:, ::-1])
    flat_hits = chosen.reshape(row_count * TOP, experts).astype(jnp.int32)
    earlier_hits = jnp.cumsum(flat_hits, 0) - flat_hits
    slot_index = jnp.sum(earlier_hits * flat_hits, -1)
    target = expert_ids.reshape(-1) * CAP + slot_index
    placed = target[:, None] == jnp.arange(experts * CAP, dtype=jnp.int32)[None, :]
    placed = placed.reshape(row_count, TOP, experts * CAP)
    selector = jnp.any(placed, 1).astype(jnp.bfloat16)
    outgoing = lax.dot_general(
        selector, normed, (((0,), (0,)), ((), ())), preferred_element_type=jnp.float32
    ).astype(jnp.bfloat16)
    outgoing = outgoing.reshape(experts, CAP, -1)
    arrived = lax.all_to_all(outgoing, "exp", split_axis=0, concat_axis=0, tiled=True)
    arrived = arrived.reshape(-1, arrived.shape[2])
    gate_part = expert_gate[0]
    up_part = expert_up[0]
    down_part = expert_down[0]
    shard_rows = lax.all_gather(arrived, "ctx", axis=0, tiled=True)
    gate_value = lax.dot_general(
        shard_rows, gate_part, (((1,), (1,)), ((), ())), preferred_element_type=jnp.float32
    )
    up_value = lax.dot_general(
        shard_rows, up_part, (((1,), (1,)), ((), ())), preferred_element_type=jnp.float32
    )
    hidden = (jax.nn.silu(gate_value) * up_value).astype(jnp.bfloat16)
    partial_out = jnp.dot(hidden, down_part, preferred_element_type=jnp.float32)
    finished = lax.psum_scatter(
        partial_out.astype(jnp.bfloat16), "ctx", scatter_dimension=0, tiled=True
    )
    returned = lax.all_to_all(
        finished.reshape(experts, CAP, -1), "exp", split_axis=0, concat_axis=0, tiled=True
    )
    returned = returned.reshape(experts * CAP, -1).astype(jnp.float32)
    combine = jnp.sum(jnp.where(placed, shares[:, :, None], 0.0), 1)
    moe_out = jnp.dot(combine, returned, precision=precise)
    return (stream + moe_out).astype(jnp.bfloat16)


def solution(mesh):
    in_specs = (
        P("ctx", "exp"),
        P("ctx", "exp"),
        P("ctx", "exp"),
        P(None, "exp"),
        P("exp"),
        P("exp", None),
        P("ctx", "exp"),
        P("exp"),
        P("exp", "ctx"),
        P(),
        P(),
        P("exp", "ctx", None),
        P("exp", "ctx", None),
        P("exp", "ctx", None),
        P(("ctx", "exp"), None),
    )
    out_specs = P(("ctx", "exp"), None)
    return jax.shard_map(local, mesh=mesh, in_specs=in_specs, out_specs=out_specs, check_vma=False)
```

profile of v0, /device:TPU:1, one launch (start us, length us, event | category | flops | bytes accessed | tf_op | source)
XLA Modules:
  0.0 636.4 jit_solution(2759990935749958650)
XLA Ops:
  6.5 0.7 all-gather.6.cloned.1.call-update
  7.3 0.7 all-gather.8.cloned.1.call-update
  8.1 0.7 all-gather.10.cloned.1.call-update
  8.8 0.5 all-gather.12.cloned.1.call-update
  9.4 0.9 fusion.53
  10.2 1.2 reduce_window_sum.22
  11.5 39.5 %all-gather.6.cloned.1.call-done = bf16[128,4096]{1,0:T(8,128)(2,1)} async-done(((bf16[128,256]{1,0:T(8,128)(2,1)}), bf16[128,4096]{1,0:T(8,128)(2,1)}) %all-gather.6.cloned.1.call-update) | async-done | bytes 1048592 | tf_op jit(solution)/shard_map/all_gather | solution.py:44
  51.0 57.7 %all-gather.8.cloned.1.call-done = bf16[4096,512]{1,0:T(8,128)(2,1)} async-done(((bf16[256,512]{1,0:T(8,128)(2,1)}), bf16[4096,512]{1,0:T(8,128)(2,1)}) %all-gather.8.cloned.1.call-update) | async-done | bytes 4194320 | tf_op jit(solution)/shard_map/all_gather | solution.py:49
  108.7 3.2 convolution_convert_fusion.4
  112.0 3.1 collective-permute-start.1
  115.1 52.4 %all-gather.10.cloned.1.call-done = bf16[4096,512]{1,0:T(8,128)(2,1)} async-done(((bf16[256,512]{1,0:T(8,128)(2,1)}), bf16[4096,512]{1,0:T(8,128)(2,1)}) %all-gather.10.cloned.1.call-update) | async-done | bytes 4194320 | tf_op jit(solution)/shard_map/all_gather | solution.py:54
  167.4 2.9 fusion.30
  170.7 46.7 %psum.7 = f32[128,32]{0,1:T(8,128)S(1)} all-reduce(f32[128,32]{0,1:T(8,128)S(1)} %fusion.54), channel_id=1, replica_groups=mesh['ctx'=16,'exp'=16] {'exp'}, use_global_device_ids=true, to_apply=%region_1.2 | all-reduce | flops 4096 | bytes 32768 | tf_op jit(solution)/shard_map/psum | solution.py:68
  217.7 0.3 fusion.31
  218.1 39.1 %while.20 = (s32[]{:T(128)}, f32[4,128,128]{2,1,0:T(8,128)S(1)}, f32[4,128,128]{2,1,0:T(8,128)S(1)}, f32[4,128,128]{2,1,0:T(8,128)S(1)}, f32[128,128]{1,0:T(8,128)S(1)}, /*index=5*/s32[]{:T(128)}) while((s32[]{:T(128)}, f32[4,128,128]{2,1,0:T(8,128)S(1)}, f32[4,128,128]{2,1,0:T(8,128)S(1)}, f32[4,128,128]{2,1,0:T(8,128)S(1)}, ...), condition=%wide.region_3.4_spmd, body=%wide.region_2.3_spmd.sunk | while | flops 35667968 | bytes 688205 | solution.py:79
  218.1 9.7 %fusion.87 = f32[128,1,128]{2,1,0:T(1,128)S(1)} fusion(f32[128,128,1]{1,2,0:T(1,128)S(1)} %bitcast.88, f32[128,128]{1,0:T(8,128)S(1)} %get-tuple-element.140, f32[128,128]{1,0:T(8,128)S(1)} %get-tuple-element.141, pred[128,128]{1,0:T(8,128)(4,1)S(1)} %iota_compare_fusion.5), kind=kOutput, calls=%fused_computation.clone.1 | convolution fusion | flops 35651584 | bytes 278528 | tf_op jit(solution)/shard_map/while/body/eval_jaxpr/ts,tsc,sc->tc/dot_general | solution.py:24
  227.9 9.7 %fusion.87 = f32[128,1,128]{2,1,0:T(1,128)S(1)} fusion(f32[128,128,1]{1,2,0:T(1,128)S(1)} %bitcast.88, f32[128,128]{1,0:T(8,128)S(1)} %get-tuple-element.140, f32[128,128]{1,0:T(8,128)S(1)} %get-tuple-element.141, pred[128,128]{1,0:T(8,128)(4,1)S(1)} %iota_compare_fusion.5), kind=kOutput, calls=%fused_computation.clone.1 | convolution fusion | flops 35651584 | bytes 278528 | tf_op jit(solution)/shard_map/while/body/eval_jaxpr/ts,tsc,sc->tc/dot_general | solution.py:24
  237.6 9.7 %fusion.87 = f32[128,1,128]{2,1,0:T(1,128)S(1)} fusion(f32[128,128,1]{1,2,0:T(1,128)S(1)} %bitcast.88, f32[128,128]{1,0:T(8,128)S(1)} %get-tuple-element.140, f32[128,128]{1,0:T(8,128)S(1)} %get-tuple-element.141, pred[128,128]{1,0:T(8,128)(4,1)S(1)} %iota_compare_fusion.5), kind=kOutput, calls=%fused_computation.clone.1 | convolution fusion | flops 35651584 | bytes 278528 | tf_op jit(solution)/shard_map/while/body/eval_jaxpr/ts,tsc,sc->tc/dot_general | solution.py:24
  247.4 9.7 %fusion.87 = f32[128,1,128]{2,1,0:T(1,128)S(1)} fusion(f32[128,128,1]{1,2,0:T(1,128)S(1)} %bitcast.88, f32[128,128]{1,0:T(8,128)S(1)} %get-tuple-element.140, f32[128,128]{1,0:T(8,128)S(1)} %get-tuple-element.141, pred[128,128]{1,0:T(8,128)(4,1)S(1)} %iota_compare_fusion.5), kind=kOutput, calls=%fused_computation.clone.1 | convolution fusion | flops 35651584 | bytes 278528 | tf_op jit(solution)/shard_map/while/body/eval_jaxpr/ts,tsc,sc->tc/dot_general | solution.py:24
  257.1 90.6 %while.21 = (s32[]{:T(128)}, f32[512,16]{0,1:T(8,128)S(1)}, f32[512]{0:T(512)S(1)}, f32[512,16]{0,1:T(8,128)S(1)}, s32[]{:T(128)}) while((s32[]{:T(128)}, f32[512,16]{0,1:T(8,128)S(1)}, f32[512]{0:T(512)S(1)}, f32[512,16]{0,1:T(8,128)S(1)}, s32[]{:T(128)}) %tuple.40), condition=%wide.region_5.6_spmd, body=%wide.region_4.5_spmd.sunk | while | flops 16386 | bytes 231525 | solution.py:92
  257.2 2.7 collective-permute-start
  259.9 1.0 collective-permute-done
  260.9 3.6 collective-permute-start
  264.5 1.0 collective-permute-done
  265.5 3.6 collective-permute-start
  269.2 1.0 collective-permute-done
  270.2 4.0 collective-permute-start
  274.3 1.0 collective-permute-done
  275.3 3.7 collective-permute-start
  279.0 1.0 collective-permute-done
  280.0 5.8 collective-permute-start
  285.8 1.0 collective-permute-done
  286.8 5.7 collective-permute-start
  292.5 1.0 collective-permute-done
  293.5 5.8 collective-permute-start
  299.3 1.0 collective-permute-done
  300.3 5.8 collective-permute-start
  306.1 1.0 collective-permute-done
  307.1 5.8 collective-permute-start
  312.8 1.0 collective-permute-done
  313.8 5.8 collective-permute-start
  319.6 1.0 collective-permute-done
  320.6 5.8 collective-permute-start
  326.4 1.2 collective-permute-done
  327.6 5.6 collective-permute-start
  333.1 1.0 collective-permute-done
  334.2 5.8 collective-permute-start
  339.9 1.0 collective-permute-done
  340.9 5.8 collective-permute-start
  346.7 1.0 collective-permute-done
  347.7 0.5 fusion.29
  348.2 3.9 convolution_convert_fusion.1
  352.9 81.0 %reduce-scatter.3.cloned.1.call-done = bf16[8,4096]{1,0:T(8,128)(2,1)} async-done(((bf16[128,4096]{1,0:T(8,128)(2,1)}), bf16[8,4096]{1,0:T(8,128)(2,1)}) %reduce-scatter.3.cloned.1.call-update) | async-done | bytes 65552 | tf_op jit(solution)/shard_map/reduce_scatter | solution.py:102
  433.9 1.0 fusion.39
  435.4 19.1 %all_to_all.10 = bf16[16,2,4096]{2,1,0:T(2,128)(2,1)S(1)} all-to-all(bf16[16,2,4096]{2,1,0:T(2,128)(2,1)S(1)} %reshape.74), channel_id=1, replica_groups=mesh['ctx'=16,'exp'=16] {'exp'}, dimensions={0} | all-to-all | bytes 524288 | tf_op jit(solution)/shard_map/all_to_all | solution.py:132
  454.5 0.8 reshape.75
  455.5 53.0 %all-gather.14.cloned.1.call-done = bf16[512,4096]{1,0:T(8,128)(2,1)} async-done(((bf16[32,4096]{1,0:T(8,128)(2,1)}), bf16[512,4096]{1,0:T(8,128)(2,1)}) %all-gather.14.cloned.1.call-update) | async-done | bytes 4194320 | tf_op jit(solution)/shard_map/all_gather | solution.py:137
  508.5 5.4 fusion.18
  513.9 10.8 %convolution_convert_fusion = bf16[512,4096]{1,0:T(8,128)(2,1)} fusion(bf16[1,448,4096]{2,1,0:T(8,128)(2,1)} %param.32, bf16[512,4096]{1,0:T(8,128)(2,1)} %all-gather.14.cloned.1.call-done, bf16[1,448,4096]{2,1,0:T(8,128)(2,1)} %param.31, f32[512,448]{0,1:T(8,128)S(1)} %fusion.18), kind=kOutput, calls=%fused_computation.19 | convolution fusion | flops 3761569792 | bytes 16646144 | tf_op jit(solution)/shard_map/dot_general | solution.py:145
  524.7 81.0 %reduce-scatter.5.cloned.1.call-done = bf16[32,4096]{1,0:T(8,128)(2,1)} async-done(((bf16[512,4096]{1,0:T(8,128)(2,1)}), bf16[32,4096]{1,0:T(8,128)(2,1)}) %reduce-scatter.5.cloned.1.call-update) | async-done | bytes 262160 | tf_op jit(solution)/shard_map/reduce_scatter | solution.py:146
  605.7 1.8 reshape.76
  607.5 9.3 %all-to-all-start.1 = ((bf16[16,2,4096]{2,1,0:T(2,128)(2,1)}), bf16[16,2,4096]{2,1,0:T(2,128)(2,1)S(1)}, u32[]{:S(2)}, u32[]{:S(2)}) async-start(bf16[16,2,4096]{2,1,0:T(2,128)(2,1)} %reshape.76), calls=%async_computation.3 | async-start | bytes 524288 | tf_op jit(solution)/shard_map/all_to_all | solution.py:149
  617.3 11.2 %all-to-all-done.1 = bf16[16,2,4096]{2,1,0:T(2,128)(2,1)S(1)} async-done(((bf16[16,2,4096]{2,1,0:T(2,128)(2,1)}), bf16[16,2,4096]{2,1,0:T(2,128)(2,1)S(1)}, u32[]{:S(2)}, u32[]{:S(2)}) %all-to-all-start.1) | async-done | bytes 262176 | tf_op jit(solution)/shard_map/all_to_all | solution.py:149
  628.7 0.9 fusion.14
  (81 shorter events, 3.3 us)
Async XLA Ops:
  6.5 610.3 %copy-start = (bf16[4096,16]{0,1:T(8,128)(2,1)S(1)}, bf16[4096,16]{0,1:T(8,128)(2,1)}, u32[]{:S(2)}) copy-start(bf16[4096,16]{0,1:T(8,128)(2,1)} %param.29) | copy-start | bytes 393220
  6.5 44.5 %all-gather.6.cloned.1.call-start = ((), (), s32[]{:S(2)}) async-start(), calls=%async_computation.4 | async-start | bytes 1114112 | tf_op jit(solution)/shard_map/all_gather | solution.py:44
  7.3 101.4 %all-gather.8.cloned.1.call-start = ((), (), s32[]{:S(2)}) async-start(), calls=%async_computation.5 | async-start | bytes 4456448 | tf_op jit(solution)/shard_map/all_gather | solution.py:49
  8.0 159.4 %all-gather.10.cloned.1.call-start = ((), (), s32[]{:S(2)}) async-start(), calls=%async_computation.6 | async-start | bytes 4456448 | tf_op jit(solution)/shard_map/all_gather | solution.py:54
  8.7 339.5 %all-gather.12.cloned.1.call-start = ((), (), s32[]{:S(2)}) async-start(), calls=%async_computation.7 | async-start | bytes 4456448 | tf_op jit(solution)/shard_map/all_gather | solution.py:101
  9.3 424.6 %reduce-scatter.3.cloned.1.call-start = ((), (), s32[]{:S(2)}) async-start(), calls=%async_computation.8 | async-start | bytes 1114112 | tf_op jit(solution)/shard_map/reduce_scatter | solution.py:102
  51.0 116.5 %copy-start.1 = (bf16[128,4096]{1,0:T(8,128)(2,1)S(1)}, bf16[128,4096]{1,0:T(8,128)(2,1)}, u32[]{:S(2)}) copy-start(bf16[128,4096]{1,0:T(8,128)(2,1)} %all-gather.6.cloned.1.call-done) | copy-start | bytes 3145732
  111.9 58.5 %copy-start.5 = (f32[512]{0:T(512)S(1)}, f32[512]{0:T(512)}, u32[]{:S(2)}) copy-start(f32[512]{0:T(512)} %param.23) | copy-start | bytes 6148
  111.9 58.7 %copy-start.2 = (bf16[512,32]{0,1:T(8,128)(2,1)S(1)}, bf16[512,32]{0,1:T(8,128)(2,1)}, u32[]{:S(2)}) copy-start(bf16[512,32]{0,1:T(8,128)(2,1)} %param.24) | copy-start | bytes 98308
  112.0 58.4 %collective-permute-start.1 = (bf16[3,512]{1,0:T(4,128)(2,1)S(1)}, bf16[3,512]{1,0:T(4,128)(2,1)S(1)}, u32[]{:S(2)}, u32[]{:S(2)}) collective-permute-start(bf16[3,512]{1,0:T(4,128)(2,1)S(1)} %slice.48), channel_id=1, source_target_pairs={{0,16},{16,32},{32,48},{48,64},{64,80},{80,96},{96,112},{112,128},... | collective-permute-start | bytes 9224 | tf_op jit(solution)/shard_map/ppermute | solution.py:16
  218.1 129.7 %copy-start.6 = (f32[512]{0:T(512)S(1)}, f32[512]{0:T(512)}, u32[]{:S(2)}) copy-start(f32[512]{0:T(512)} %param.26) | copy-start | bytes 6148
  257.2 3.7 collective-permute-start
  260.9 4.7 collective-permute-start
  265.5 4.7 collective-permute-start
  270.2 5.1 collective-permute-start
  275.3 4.7 collective-permute-start
  280.0 6.9 %collective-permute-start = (f32[512,16]{0,1:T(8,128)S(1)}, f32[512,16]{0,1:T(8,128)S(1)}, u32[]{:S(2)}, u32[]{:S(2)}) collective-permute-start(f32[512,16]{0,1:T(8,128)S(1)} %multiply_add_fusion.3), channel_id=1, source_target_pairs={{0,16},{16,32},{32,48},{48,64},{64,80},{80,96},{96,112},{112,128},... | collective-permute-start | bytes 98312 | tf_op jit(solution)/shard_map/while/body/eval_jaxpr/ppermute | solution.py:16
  286.8 6.7 %collective-permute-start = (f32[512,16]{0,1:T(8,128)S(1)}, f32[512,16]{0,1:T(8,128)S(1)}, u32[]{:S(2)}, u32[]{:S(2)}) collective-permute-start(f32[512,16]{0,1:T(8,128)S(1)} %multiply_add_fusion.3), channel_id=1, source_target_pairs={{0,16},{16,32},{32,48},{48,64},{64,80},{80,96},{96,112},{112,128},... | collective-permute-start | bytes 98312 | tf_op jit(solution)/shard_map/while/body/eval_jaxpr/ppermute | solution.py:16
  293.5 6.8 %collective-permute-start = (f32[512,16]{0,1:T(8,128)S(1)}, f32[512,16]{0,1:T(8,128)S(1)}, u32[]{:S(2)}, u32[]{:S(2)}) collective-permute-start(f32[512,16]{0,1:T(8,128)S(1)} %multiply_add_fusion.3), channel_id=1, source_target_pairs={{0,16},{16,32},{32,48},{48,64},{64,80},{80,96},{96,112},{112,128},... | collective-permute-start | bytes 98312 | tf_op jit(solution)/shard_map/while/body/eval_jaxpr/ppermute | solution.py:16
  300.3 6.8 %collective-permute-start = (f32[512,16]{0,1:T(8,128)S(1)}, f32[512,16]{0,1:T(8,128)S(1)}, u32[]{:S(2)}, u32[]{:S(2)}) collective-permute-start(f32[512,16]{0,1:T(8,128)S(1)} %multiply_add_fusion.3), channel_id=1, source_target_pairs={{0,16},{16,32},{32,48},{48,64},{64,80},{80,96},{96,112},{112,128},... | collective-permute-start | bytes 98312 | tf_op jit(solution)/shard_map/while/body/eval_jaxpr/ppermute | solution.py:16
  307.1 6.8 %collective-permute-start = (f32[512,16]{0,1:T(8,128)S(1)}, f32[512,16]{0,1:T(8,128)S(1)}, u32[]{:S(2)}, u32[]{:S(2)}) collective-permute-start(f32[512,16]{0,1:T(8,128)S(1)} %multiply_add_fusion.3), channel_id=1, source_target_pairs={{0,16},{16,32},{32,48},{48,64},{64,80},{80,96},{96,112},{112,128},... | collective-permute-start | bytes 98312 | tf_op jit(solution)/shard_map/while/body/eval_jaxpr/ppermute | solution.py:16
  313.8 6.8 %collective-permute-start = (f32[512,16]{0,1:T(8,128)S(1)}, f32[512,16]{0,1:T(8,128)S(1)}, u32[]{:S(2)}, u32[]{:S(2)}) collective-permute-start(f32[512,16]{0,1:T(8,128)S(1)} %multiply_add_fusion.3), channel_id=1, source_target_pairs={{0,16},{16,32},{32,48},{48,64},{64,80},{80,96},{96,112},{112,128},... | collective-permute-start | bytes 98312 | tf_op jit(solution)/shard_map/while/body/eval_jaxpr/ppermute | solution.py:16
  320.6 6.9 %collective-permute-start = (f32[512,16]{0,1:T(8,128)S(1)}, f32[512,16]{0,1:T(8,128)S(1)}, u32[]{:S(2)}, u32[]{:S(2)}) collective-permute-start(f32[512,16]{0,1:T(8,128)S(1)} %multiply_add_fusion.3), channel_id=1, source_target_pairs={{0,16},{16,32},{32,48},{48,64},{64,80},{80,96},{96,112},{112,128},... | collective-permute-start | bytes 98312 | tf_op jit(solution)/shard_map/while/body/eval_jaxpr/ppermute | solution.py:16
  327.6 6.6 %collective-permute-start = (f32[512,16]{0,1:T(8,128)S(1)}, f32[512,16]{0,1:T(8,128)S(1)}, u32[]{:S(2)}, u32[]{:S(2)}) collective-permute-start(f32[512,16]{0,1:T(8,128)S(1)} %multiply_add_fusion.3), channel_id=1, source_target_pairs={{0,16},{16,32},{32,48},{48,64},{64,80},{80,96},{96,112},{112,128},... | collective-permute-start | bytes 98312 | tf_op jit(solution)/shard_map/while/body/eval_jaxpr/ppermute | solution.py:16
  334.2 6.8 %collective-permute-start = (f32[512,16]{0,1:T(8,128)S(1)}, f32[512,16]{0,1:T(8,128)S(1)}, u32[]{:S(2)}, u32[]{:S(2)}) collective-permute-start(f32[512,16]{0,1:T(8,128)S(1)} %multiply_add_fusion.3), channel_id=1, source_target_pairs={{0,16},{16,32},{32,48},{48,64},{64,80},{80,96},{96,112},{112,128},... | collective-permute-start | bytes 98312 | tf_op jit(solution)/shard_map/while/body/eval_jaxpr/ppermute | solution.py:16
  340.9 6.8 %collective-permute-start = (f32[512,16]{0,1:T(8,128)S(1)}, f32[512,16]{0,1:T(8,128)S(1)}, u32[]{:S(2)}, u32[]{:S(2)}) collective-permute-start(f32[512,16]{0,1:T(8,128)S(1)} %multiply_add_fusion.3), channel_id=1, source_target_pairs={{0,16},{16,32},{32,48},{48,64},{64,80},{80,96},{96,112},{112,128},... | collective-permute-start | bytes 98312 | tf_op jit(solution)/shard_map/while/body/eval_jaxpr/ppermute | solution.py:16
  347.7 4.5 copy-start.4
  347.7 87.2 %copy-start.3 = (f32[4096]{0:T(1024)S(1)}, f32[4096]{0:T(1024)}, u32[]{:S(2)}) copy-start(f32[4096]{0:T(1024)} %param.28) | copy-start | bytes 49156
  352.1 156.4 %all-gather.14.cloned.1.call-start = ((), (), s32[]{:S(2)}) async-start(), calls=%async_computation.9 | async-start | bytes 4456448 | tf_op jit(solution)/shard_map/all_gather | solution.py:137
  455.3 150.4 %reduce-scatter.5.cloned.1.call-start = ((), (), s32[]{:S(2)}) async-start(), calls=%async_computation.10 | async-start | bytes 4456448 | tf_op jit(solution)/shard_map/reduce_scatter | solution.py:146
  607.5 21.1 %all-to-all-start.1 = ((bf16[16,2,4096]{2,1,0:T(2,128)(2,1)}), bf16[16,2,4096]{2,1,0:T(2,128)(2,1)S(1)}, u32[]{:S(2)}, u32[]{:S(2)}) async-start(bf16[16,2,4096]{2,1,0:T(2,128)(2,1)} %reshape.76), calls=%async_computation.3 | async-start | bytes 524288 | tf_op jit(solution)/shard_map/all_to_all | solution.py:149
Sparse Core Ops, SparseCore 0:
  9.1 41.8 all-gather.5
  53.4 55.2 all-gather.7
  111.1 56.2 all-gather.9
  169.7 61.4 all-gather.11
  352.2 81.6 reduce-scatter.2
  455.4 53.0 all-gather.13
  524.8 80.7 reduce-scatter.4
where the time goes:
time: 637 us; the launch traced here: 636 us
  waiting for transfers between devices  394 us (62%)
  starting transfers between devices  87.9 us (14%)
  matrix products  67.4 us (11%)
  blocking collectives  65.7 us (10%)
  between operations  13.7 us (2%)
    reduce_scatter x1, waiting for transfers between devices, local(): lax.psum_scatter(jnp.dot(blender_result, out_whole, preferred_element_typ...  81 us
    reduce_scatter x1, waiting for transfers between devices, local(): lax.psum_scatter(partial_out.astype(jnp.bfloat16), 'ctx', scatter_dimensi...  81 us
    ppermute x16, starting transfers between devices, shifted(): return lax.ppermute(shard, axis, pairs)  78.2 us
    all_gather x1, waiting for transfers between devices, local(): lax.all_gather(input_weight, 'ctx', axis=0, tiled=True)  57.7 us
    all_gather x1, waiting for transfers between devices, local(): shard_rows = lax.all_gather(arrived, 'ctx', axis=0, tiled=True)  53 us
    all_gather x1, waiting for transfers between devices, local(): lax.all_gather(gate_weight, 'ctx', axis=0, tiled=True)  52.4 us
    psum x1, blocking collectives, local(): lax.psum(jnp.dot(mixer_in, state_weight, preferred_element_type=jnp.float...  46.7 us
    all_gather x1, waiting for transfers between devices, local(): whole_stretch = lax.all_gather(tokens, 'exp', axis=1, tiled=True)  39.5 us
  transfers between devices with their start and end apart: 24, of which 22 were waited for; matrix products, arithmetic and copies ran while one was open for 8% of the time, Pallas kernels for 0%

commit v1 on v0

--- a/solution.py
+++ b/solution.py
@@ -41,7 +41,12 @@
     expert_down,
     expert_ids,
 ):
-    whole_stretch = lax.all_gather(tokens, "exp", axis=1, tiled=True)
+    ring = [tokens]
+    for hop in range(15):
+        ring.append(lax.ppermute(ring[-1], "exp", [(dev, (dev + 1) % 16) for dev in range(16)]))
+    whole_stretch = jnp.roll(
+        jnp.concatenate(ring[::-1], axis=1), (lax.axis_index("exp") + 1) * ring[0].shape[1], axis=1
+    )
     stretch_rows = whole_stretch.shape[0]
     inner_width = input_weight.shape[1]
     inner_x = jnp.dot(

time: 637 us -> 603 us (0.947)
  waiting for transfers between devices: 394 us -> 348 us
  starting transfers between devices: 87.9 us -> 94.3 us
    ppermute x0 -> x15, waiting for transfers between devices: none -> 64.5 us  [local(): lax.ppermute(ring[-1], 'exp', [(dev, (dev + 1) % 16) for dev in range(16)])]
    all_gather x1, waiting for transfers between devices: 57.7 us -> 0.02 us  [local(): lax.all_gather(input_weight, 'ctx', axis=0, tiled=True)]
    all_gather x1 -> x0, waiting for transfers between devices: 39.5 us -> none  [local(): whole_stretch = lax.all_gather(tokens, 'exp', axis=1, tiled=True)]
    all_gather x1, waiting for transfers between devices: 52.4 us -> 40.7 us  [local(): lax.all_gather(gate_weight, 'ctx', axis=0, tiled=True)]
  transfers between devices with their start and end apart: 24 -> 38, of which waited for: 22 -> 35; matrix products, arithmetic and copies ran while one was open for 8% -> 9% of each run, Pallas kernels for 0% -> 0%
where the time goes in v1:
time: 603 us; the launch traced here: 602 us
  waiting for transfers between devices  348 us (58%)
  starting transfers between devices  94.3 us (16%)
  matrix products  68.8 us (11%)
  blocking collectives  65.5 us (11%)
  between operations  14 us (2%)
  local copies, waits for them, and re-layouts  7.66 us (1%)
    reduce_scatter x1, waiting for transfers between devices, local(): lax.psum_scatter(jnp.dot(blender_result, out_whole, preferred_element_typ...  81.2 us
    reduce_scatter x1, waiting for transfers between devices, local(): lax.psum_scatter(partial_out.astype(jnp.bfloat16), 'ctx', scatter_dimensi...  80.9 us
    ppermute x16, starting transfers between devices, shifted(): return lax.ppermute(shard, axis, pairs)  78.3 us
    ppermute x15, waiting for transfers between devices, local(): lax.ppermute(ring[-1], 'exp', [(dev, (dev + 1) % 16) for dev in range(16)])  64.5 us
    all_gather x1, waiting for transfers between devices, local(): shard_rows = lax.all_gather(arrived, 'ctx', axis=0, tiled=True)  53 us
    psum x1, blocking collectives, local(): lax.psum(jnp.dot(mixer_in, state_weight, preferred_element_type=jnp.float...  46.3 us
    all_gather x1, waiting for transfers between devices, local(): lax.all_gather(gate_weight, 'ctx', axis=0, tiled=True)  40.7 us
    dot_general x4, matrix products, causal_part(): jnp.einsum('ts,tsc,sc->tc', scores, weight, input_block, precision=precise)  38.7 us
  transfers between devices with their start and end apart: 38, of which 35 were waited for; matrix products, arithmetic and copies ran while one was open for 9% of the time, Pallas kernels for 0%

profile of v1, /device:TPU:1, one launch (start us, length us, event | category | flops | bytes accessed | tf_op | source)
XLA Modules:
  0.0 602.0 jit_solution(902552096561392449)
XLA Ops:
  8.1 3.0 collective-permute-start.1
  11.1 1.6 collective-permute-done.1
  12.7 2.3 collective-permute-start.2
  15.0 2.8 collective-permute-done.2
  18.7 4.0 collective-permute-done.3
  22.7 4.9 collective-permute-done.4
  27.6 4.9 collective-permute-done.5
  32.5 4.9 collective-permute-done.6
  37.4 4.9 collective-permute-done.7
  42.3 4.9 collective-permute-done.8
  47.2 4.9 collective-permute-done.9
  52.1 4.9 collective-permute-done.10
  57.0 4.9 collective-permute-done.11
  61.9 4.9 collective-permute-done.12
  66.9 4.8 collective-permute-done.13
  71.7 1.4 fusion.57
  73.1 1.2 reduce_window_sum.22
  74.4 2.3 collective-permute-done.14
  76.6 4.9 collective-permute-done.15
  82.0 2.9 convolution_convert_fusion.4
  85.0 3.2 collective-permute-start.16
  88.2 40.7 %all-gather.7.cloned.1.call-done = bf16[4096,512]{1,0:T(8,128)(2,1)} async-done(((bf16[256,512]{1,0:T(8,128)(2,1)}), bf16[4096,512]{1,0:T(8,128)(2,1)}) %all-gather.7.cloned.1.call-update) | async-done | bytes 4194320 | tf_op jit(solution)/shard_map/all_gather | solution.py:59
  128.9 3.6 fusion.30
  132.9 46.3 %psum.7 = f32[128,32]{0,1:T(8,128)S(1)} all-reduce(f32[128,32]{0,1:T(8,128)S(1)} %fusion.58), channel_id=1, replica_groups=mesh['ctx'=16,'exp'=16] {'exp'}, use_global_device_ids=true, to_apply=%region_1.2 | all-reduce | flops 4096 | bytes 32768 | tf_op jit(solution)/shard_map/psum | solution.py:73
  179.9 41.4 %while.20 = (s32[]{:T(128)}, f32[4,128,128]{2,1,0:T(8,128)}, f32[4,128,128]{2,1,0:T(8,128)S(1)}, f32[4,128,128]{2,1,0:T(8,128)S(1)}, f32[128,128]{1,0:T(8,128)S(1)}, /*index=5*/s32[]{:T(128)}) while((s32[]{:T(128)}, f32[4,128,128]{2,1,0:T(8,128)}, f32[4,128,128]{2,1,0:T(8,128)S(1)}, f32[4,128,128]{2,1,0:T(8,128)S(1)}, ...), condition=%wide.region_3.4_spmd, body=%wide.region_2.3_spmd.sunk | while | flops 35667968 | bytes 688713 | solution.py:84
  179.9 9.7 %fusion.89 = f32[128,1,128]{2,1,0:T(1,128)S(1)} fusion(f32[128,128,1]{1,2,0:T(1,128)S(1)} %bitcast.86, f32[128,128]{1,0:T(8,128)S(1)} %get-tuple-element.140, f32[128,128]{1,0:T(8,128)S(1)} %get-tuple-element.141, pred[128,128]{1,0:T(8,128)(4,1)S(1)} %iota_compare_fusion.5), kind=kOutput, calls=%fused_computation.clone.1 | convolution fusion | flops 35651584 | bytes 278528 | tf_op jit(solution)/shard_map/while/body/eval_jaxpr/ts,tsc,sc->tc/dot_general | solution.py:24
  190.3 9.7 %fusion.89 = f32[128,1,128]{2,1,0:T(1,128)S(1)} fusion(f32[128,128,1]{1,2,0:T(1,128)S(1)} %bitcast.86, f32[128,128]{1,0:T(8,128)S(1)} %get-tuple-element.140, f32[128,128]{1,0:T(8,128)S(1)} %get-tuple-element.141, pred[128,128]{1,0:T(8,128)(4,1)S(1)} %iota_compare_fusion.5), kind=kOutput, calls=%fused_computation.clone.1 | convolution fusion | flops 35651584 | bytes 278528 | tf_op jit(solution)/shard_map/while/body/eval_jaxpr/ts,tsc,sc->tc/dot_general | solution.py:24
  200.6 9.7 %fusion.89 = f32[128,1,128]{2,1,0:T(1,128)S(1)} fusion(f32[128,128,1]{1,2,0:T(1,128)S(1)} %bitcast.86, f32[128,128]{1,0:T(8,128)S(1)} %get-tuple-element.140, f32[128,128]{1,0:T(8,128)S(1)} %get-tuple-element.141, pred[128,128]{1,0:T(8,128)(4,1)S(1)} %iota_compare_fusion.5), kind=kOutput, calls=%fused_computation.clone.1 | convolution fusion | flops 35651584 | bytes 278528 | tf_op jit(solution)/shard_map/while/body/eval_jaxpr/ts,tsc,sc->tc/dot_general | solution.py:24
  211.0 9.7 %fusion.89 = f32[128,1,128]{2,1,0:T(1,128)S(1)} fusion(f32[128,128,1]{1,2,0:T(1,128)S(1)} %bitcast.86, f32[128,128]{1,0:T(8,128)S(1)} %get-tuple-element.140, f32[128,128]{1,0:T(8,128)S(1)} %get-tuple-element.141, pred[128,128]{1,0:T(8,128)(4,1)S(1)} %iota_compare_fusion.5), kind=kOutput, calls=%fused_computation.clone.1 | convolution fusion | flops 35651584 | bytes 278528 | tf_op jit(solution)/shard_map/while/body/eval_jaxpr/ts,tsc,sc->tc/dot_general | solution.py:24
  221.3 90.6 %while.21 = (s32[]{:T(128)}, f32[512,16]{0,1:T(8,128)S(1)}, f32[512]{0:T(512)S(1)}, f32[512,16]{0,1:T(8,128)S(1)}, s32[]{:T(128)}) while((s32[]{:T(128)}, f32[512,16]{0,1:T(8,128)S(1)}, f32[512]{0:T(512)S(1)}, f32[512,16]{0,1:T(8,128)S(1)}, s32[]{:T(128)}) %tuple.40), condition=%wide.region_5.6_spmd, body=%wide.region_4.5_spmd.sunk | while | flops 16386 | bytes 231525 | solution.py:97
  221.3 2.7 collective-permute-start
  224.0 1.0 collective-permute-done
  225.0 3.6 collective-permute-start
  228.7 1.0 collective-permute-done
  229.7 3.6 collective-permute-start
  234.4 3.6 collective-permute-start
  238.0 1.0 collective-permute-done
  239.0 4.1 collective-permute-start
  243.2 1.0 collective-permute-done
  244.2 5.8 collective-permute-start
  250.0 1.0 collective-permute-done
  251.0 5.7 collective-permute-start
  256.7 1.0 collective-permute-done
  257.7 5.8 collective-permute-start
  264.5 5.8 collective-permute-start
  271.2 5.8 collective-permute-start
  278.0 5.8 collective-permute-start
  284.8 5.8 collective-permute-start
  290.6 1.2 collective-permute-done
  291.7 5.6 collective-permute-start
  298.3 5.8 collective-permute-start
  305.1 5.8 collective-permute-start
  311.9 1.4 fusion.29
  313.4 3.9 convolution_convert_fusion.1
  318.1 81.2 %reduce-scatter.3.cloned.1.call-done = bf16[8,4096]{1,0:T(8,128)(2,1)} async-done(((bf16[128,4096]{1,0:T(8,128)(2,1)}), bf16[8,4096]{1,0:T(8,128)(2,1)}) %reduce-scatter.3.cloned.1.call-update) | async-done | bytes 65552 | tf_op jit(solution)/shard_map/reduce_scatter | solution.py:107
  399.3 1.1 fusion.41
  400.9 19.3 %all_to_all.10 = bf16[16,2,4096]{2,1,0:T(2,128)(2,1)S(1)} all-to-all(bf16[16,2,4096]{2,1,0:T(2,128)(2,1)S(1)} %reshape.74), channel_id=1, replica_groups=mesh['ctx'=16,'exp'=16] {'exp'}, dimensions={0} | all-to-all | bytes 524288 | tf_op jit(solution)/shard_map/all_to_all | solution.py:137
  421.2 53.0 %all-gather.11.cloned.1.call-done = bf16[512,4096]{1,0:T(8,128)(2,1)} async-done(((bf16[32,4096]{1,0:T(8,128)(2,1)}), bf16[512,4096]{1,0:T(8,128)(2,1)}) %all-gather.11.cloned.1.call-update) | async-done | bytes 4194320 | tf_op jit(solution)/shard_map/all_gather | solution.py:142
  474.2 5.4 fusion.18
  479.6 10.8 %convolution_convert_fusion = bf16[512,4096]{1,0:T(8,128)(2,1)} fusion(bf16[1,448,4096]{2,1,0:T(8,128)(2,1)} %param.32, bf16[512,4096]{1,0:T(8,128)(2,1)} %all-gather.11.cloned.1.call-done, bf16[1,448,4096]{2,1,0:T(8,128)(2,1)} %param.31, f32[512,448]{0,1:T(8,128)S(1)} %fusion.18), kind=kOutput, calls=%fused_computation.19 | convolution fusion | flops 3761569792 | bytes 16646144 | tf_op jit(solution)/shard_map/dot_general | solution.py:150
  490.4 80.9 %reduce-scatter.5.cloned.1.call-done = bf16[32,4096]{1,0:T(8,128)(2,1)} async-done(((bf16[512,4096]{1,0:T(8,128)(2,1)}), bf16[32,4096]{1,0:T(8,128)(2,1)}) %reduce-scatter.5.cloned.1.call-update) | async-done | bytes 262160 | tf_op jit(solution)/shard_map/reduce_scatter | solution.py:151
  571.3 1.8 reshape.76
  573.2 9.3 %all-to-all-start.1 = ((bf16[16,2,4096]{2,1,0:T(2,128)(2,1)}), bf16[16,2,4096]{2,1,0:T(2,128)(2,1)S(1)}, u32[]{:S(2)}, u32[]{:S(2)}) async-start(bf16[16,2,4096]{2,1,0:T(2,128)(2,1)} %reshape.76), calls=%async_computation.3 | async-start | bytes 524288 | tf_op jit(solution)/shard_map/all_to_all | solution.py:154
  583.0 11.2 %all-to-all-done.1 = bf16[16,2,4096]{2,1,0:T(2,128)(2,1)S(1)} async-done(((bf16[16,2,4096]{2,1,0:T(2,128)(2,1)}), bf16[16,2,4096]{2,1,0:T(2,128)(2,1)S(1)}, u32[]{:S(2)}, u32[]{:S(2)}) %all-to-all-start.1) | async-done | bytes 262176 | tf_op jit(solution)/shard_map/all_to_all | solution.py:154
  (146 shorter events, 18.3 us)
Async XLA Ops:
  6.5 576.0 %copy-start = (bf16[4096,16]{0,1:T(8,128)(2,1)S(1)}, bf16[4096,16]{0,1:T(8,128)(2,1)}, u32[]{:S(2)}) copy-start(bf16[4096,16]{0,1:T(8,128)(2,1)} %param.29) | copy-start | bytes 393220
  6.5 75.2 %copy-start.2 = (bf16[128,256]{1,0:T(8,128)(2,1)S(1)}, bf16[128,256]{1,0:T(8,128)(2,1)}, u32[]{:S(2)}) copy-start(bf16[128,256]{1,0:T(8,128)(2,1)} %param.19) | copy-start | bytes 196612
  6.5 75.5 %all-gather.5.cloned.1.call-start = ((), (), s32[]{:S(2)}) async-start(), calls=%async_computation.4 | async-start | bytes 4456448 | tf_op jit(solution)/shard_map/all_gather | solution.py:54
  7.3 121.7 %all-gather.7.cloned.1.call-start = ((), (), s32[]{:S(2)}) async-start(), calls=%async_computation.5 | async-start | bytes 4456448 | tf_op jit(solution)/shard_map/all_gather | solution.py:59
  8.0 305.3 %all-gather.9.cloned.1.call-start = ((), (), s32[]{:S(2)}) async-start(), calls=%async_computation.6 | async-start | bytes 4456448 | tf_op jit(solution)/shard_map/all_gather | solution.py:106
  8.1 4.7 collective-permute-start.1
  12.7 5.0 collective-permute-start.2
  17.8 4.9 collective-permute-start.3
  22.7 4.9 collective-permute-start.4
  27.6 4.9 collective-permute-start.5
  32.5 4.9 collective-permute-start.6
  37.4 4.9 collective-permute-start.7
  42.3 4.9 collective-permute-start.8
  47.2 4.9 collective-permute-start.9
  52.1 4.9 collective-permute-start.10
  57.0 4.9 collective-permute-start.11
  61.9 4.9 collective-permute-start.12
  66.8 4.9 collective-permute-start.13
  66.8 332.5 %reduce-scatter.3.cloned.1.call-start = ((), (), s32[]{:S(2)}) async-start(), calls=%async_computation.7 | async-start | bytes 1114112 | tf_op jit(solution)/shard_map/reduce_scatter | solution.py:107
  71.7 4.9 collective-permute-start.14
  76.6 4.9 collective-permute-start.15
  84.9 47.7 %copy-start.5 = (f32[1,512]{1,0:T(1,128)S(1)}, f32[1,512]{1,0:T(1,128)}, u32[]{:S(2)}) copy-start(f32[1,512]{1,0:T(1,128)} %get-tuple-element.82) | copy-start | bytes 6148
  84.9 47.6 %copy-start.6 = (f32[1,512]{1,0:T(1,128)S(1)}, f32[1,512]{1,0:T(1,128)}, u32[]{:S(2)}) copy-start(f32[1,512]{1,0:T(1,128)} %get-tuple-element.83) | copy-start | bytes 6148
  84.9 47.6 %copy-start.8 = (f32[512]{0:T(512)S(1)}, f32[512]{0:T(512)}, u32[]{:S(2)}) copy-start(f32[512]{0:T(512)} %param.23) | copy-start | bytes 6148
  85.0 47.8 %copy-start.3 = (bf16[512,32]{0,1:T(8,128)(2,1)S(1)}, bf16[512,32]{0,1:T(8,128)(2,1)}, u32[]{:S(2)}) copy-start(bf16[512,32]{0,1:T(8,128)(2,1)} %param.24) | copy-start | bytes 98308
  85.0 47.6 %collective-permute-start.16 = (bf16[3,512]{1,0:T(4,128)(2,1)S(1)}, bf16[3,512]{1,0:T(4,128)(2,1)S(1)}, u32[]{:S(2)}, u32[]{:S(2)}) collective-permute-start(bf16[3,512]{1,0:T(4,128)(2,1)S(1)} %slice.48), channel_id=1, source_target_pairs={{0,16},{16,32},{32,48},{48,64},{64,80},{80,96},{96,112},{112,128},... | collective-permute-start | bytes 9224 | tf_op jit(solution)/shard_map/ppermute | solution.py:16
  179.8 132.0 %copy-start.1 = (f32[128,512]{1,0:T(8,128)S(1)}, f32[128,512]{1,0:T(8,128)}, u32[]{:S(2)}) copy-start(f32[128,512]{1,0:T(8,128)} %fusion.30) | copy-start | bytes 786436
  179.9 132.0 %copy-start.9 = (f32[512]{0:T(512)S(1)}, f32[512]{0:T(512)}, u32[]{:S(2)}) copy-start(f32[512]{0:T(512)} %param.26) | copy-start | bytes 6148
  221.3 3.7 collective-permute-start
  225.0 4.7 collective-permute-start
  229.7 4.7 collective-permute-start
  234.4 4.7 collective-permute-start
  239.0 5.1 collective-permute-start
  244.2 6.9 %collective-permute-start = (f32[512,16]{0,1:T(8,128)S(1)}, f32[512,16]{0,1:T(8,128)S(1)}, u32[]{:S(2)}, u32[]{:S(2)}) collective-permute-start(f32[512,16]{0,1:T(8,128)S(1)} %multiply_add_fusion.3), channel_id=1, source_target_pairs={{0,16},{16,32},{32,48},{48,64},{64,80},{80,96},{96,112},{112,128},... | collective-permute-start | bytes 98312 | tf_op jit(solution)/shard_map/while/body/eval_jaxpr/ppermute | solution.py:16
  251.0 6.7 %collective-permute-start = (f32[512,16]{0,1:T(8,128)S(1)}, f32[512,16]{0,1:T(8,128)S(1)}, u32[]{:S(2)}, u32[]{:S(2)}) collective-permute-start(f32[512,16]{0,1:T(8,128)S(1)} %multiply_add_fusion.3), channel_id=1, source_target_pairs={{0,16},{16,32},{32,48},{48,64},{64,80},{80,96},{96,112},{112,128},... | collective-permute-start | bytes 98312 | tf_op jit(solution)/shard_map/while/body/eval_jaxpr/ppermute | solution.py:16
  257.7 6.8 %collective-permute-start = (f32[512,16]{0,1:T(8,128)S(1)}, f32[512,16]{0,1:T(8,128)S(1)}, u32[]{:S(2)}, u32[]{:S(2)}) collective-permute-start(f32[512,16]{0,1:T(8,128)S(1)} %multiply_add_fusion.3), channel_id=1, source_target_pairs={{0,16},{16,32},{32,48},{48,64},{64,80},{80,96},{96,112},{112,128},... | collective-permute-start | bytes 98312 | tf_op jit(solution)/shard_map/while/body/eval_jaxpr/ppermute | solution.py:16
  264.5 6.8 %collective-permute-start = (f32[512,16]{0,1:T(8,128)S(1)}, f32[512,16]{0,1:T(8,128)S(1)}, u32[]{:S(2)}, u32[]{:S(2)}) collective-permute-start(f32[512,16]{0,1:T(8,128)S(1)} %multiply_add_fusion.3), channel_id=1, source_target_pairs={{0,16},{16,32},{32,48},{48,64},{64,80},{80,96},{96,112},{112,128},... | collective-permute-start | bytes 98312 | tf_op jit(solution)/shard_map/while/body/eval_jaxpr/ppermute | solution.py:16
  271.2 6.8 %collective-permute-start = (f32[512,16]{0,1:T(8,128)S(1)}, f32[512,16]{0,1:T(8,128)S(1)}, u32[]{:S(2)}, u32[]{:S(2)}) collective-permute-start(f32[512,16]{0,1:T(8,128)S(1)} %multiply_add_fusion.3), channel_id=1, source_target_pairs={{0,16},{16,32},{32,48},{48,64},{64,80},{80,96},{96,112},{112,128},... | collective-permute-start | bytes 98312 | tf_op jit(solution)/shard_map/while/body/eval_jaxpr/ppermute | solution.py:16
  278.0 6.8 %collective-permute-start = (f32[512,16]{0,1:T(8,128)S(1)}, f32[512,16]{0,1:T(8,128)S(1)}, u32[]{:S(2)}, u32[]{:S(2)}) collective-permute-start(f32[512,16]{0,1:T(8,128)S(1)} %multiply_add_fusion.3), channel_id=1, source_target_pairs={{0,16},{16,32},{32,48},{48,64},{64,80},{80,96},{96,112},{112,128},... | collective-permute-start | bytes 98312 | tf_op jit(solution)/shard_map/while/body/eval_jaxpr/ppermute | solution.py:16
  284.8 6.9 %collective-permute-start = (f32[512,16]{0,1:T(8,128)S(1)}, f32[512,16]{0,1:T(8,128)S(1)}, u32[]{:S(2)}, u32[]{:S(2)}) collective-permute-start(f32[512,16]{0,1:T(8,128)S(1)} %multiply_add_fusion.3), channel_id=1, source_target_pairs={{0,16},{16,32},{32,48},{48,64},{64,80},{80,96},{96,112},{112,128},... | collective-permute-start | bytes 98312 | tf_op jit(solution)/shard_map/while/body/eval_jaxpr/ppermute | solution.py:16
  291.7 6.6 %collective-permute-start = (f32[512,16]{0,1:T(8,128)S(1)}, f32[512,16]{0,1:T(8,128)S(1)}, u32[]{:S(2)}, u32[]{:S(2)}) collective-permute-start(f32[512,16]{0,1:T(8,128)S(1)} %multiply_add_fusion.3), channel_id=1, source_target_pairs={{0,16},{16,32},{32,48},{48,64},{64,80},{80,96},{96,112},{112,128},... | collective-permute-start | bytes 98312 | tf_op jit(solution)/shard_map/while/body/eval_jaxpr/ppermute | solution.py:16
  298.3 6.8 %collective-permute-start = (f32[512,16]{0,1:T(8,128)S(1)}, f32[512,16]{0,1:T(8,128)S(1)}, u32[]{:S(2)}, u32[]{:S(2)}) collective-permute-start(f32[512,16]{0,1:T(8,128)S(1)} %multiply_add_fusion.3), channel_id=1, source_target_pairs={{0,16},{16,32},{32,48},{48,64},{64,80},{80,96},{96,112},{112,128},... | collective-permute-start | bytes 98312 | tf_op jit(solution)/shard_map/while/body/eval_jaxpr/ppermute | solution.py:16
  305.1 6.8 %collective-permute-start = (f32[512,16]{0,1:T(8,128)S(1)}, f32[512,16]{0,1:T(8,128)S(1)}, u32[]{:S(2)}, u32[]{:S(2)}) collective-permute-start(f32[512,16]{0,1:T(8,128)S(1)} %multiply_add_fusion.3), channel_id=1, source_target_pairs={{0,16},{16,32},{32,48},{48,64},{64,80},{80,96},{96,112},{112,128},... | collective-permute-start | bytes 98312 | tf_op jit(solution)/shard_map/while/body/eval_jaxpr/ppermute | solution.py:16
  313.3 4.1 copy-start.7
  313.3 87.1 %copy-start.4 = (f32[4096]{0:T(1024)S(1)}, f32[4096]{0:T(1024)}, u32[]{:S(2)}) copy-start(f32[4096]{0:T(1024)} %param.28) | copy-start | bytes 49156
  317.3 156.9 %all-gather.11.cloned.1.call-start = ((), (), s32[]{:S(2)}) async-start(), calls=%async_computation.8 | async-start | bytes 4456448 | tf_op jit(solution)/shard_map/all_gather | solution.py:142
  421.0 150.4 %reduce-scatter.5.cloned.1.call-start = ((), (), s32[]{:S(2)}) async-start(), calls=%async_computation.9 | async-start | bytes 4456448 | tf_op jit(solution)/shard_map/reduce_scatter | solution.py:151
  573.2 21.1 %all-to-all-start.1 = ((bf16[16,2,4096]{2,1,0:T(2,128)(2,1)}), bf16[16,2,4096]{2,1,0:T(2,128)(2,1)S(1)}, u32[]{:S(2)}, u32[]{:S(2)}) async-start(bf16[16,2,4096]{2,1,0:T(2,128)(2,1)} %reshape.76), calls=%async_computation.3 | async-start | bytes 524288 | tf_op jit(solution)/shard_map/all_to_all | solution.py:154
Sparse Core Ops, SparseCore 0:
  9.8 60.3 all-gather.4
  72.6 56.2 all-gather.6
  131.3 61.4 all-gather.8
  317.4 81.8 reduce-scatter.2
  421.1 53.0 all-gather.10
  490.5 80.7 reduce-scatter.4
